TPU v7x, 32 devices: a whole 2x2x4 slice. The times are simulated.
32 devices in a mesh: batch: 2 (over x), seq: 4 (over y, core), mp: 4 (over z).
Axes of the slice: x: 2, y: 2, z: 4, core: 2. Of those that a mesh axis runs over, the one named last changes fastest.
Arguments:
- context: bfloat16 [1024, 6144], P(('batch', 'seq'), 'mp'), may hold values from -0.25 to 0.25
- cotangent: bfloat16 [1024, 6144], P(('batch', 'seq'), 'mp'), may hold values from -6 to 6
- out_weight: bfloat16 [6144, 6144], P(None, 'mp'), may hold values from -0.078125 to 0.078125
Outputs:
- grad_weight: float32 [6144, 6144], P(('batch', 'seq'), 'mp')
- grad_context: bfloat16 [1024, 6144], P(('batch', 'seq'), 'mp')
All inputs are finite; a program needn't handle non-finite values.
Results may differ from a plain program's by a relative error of at most 0.001.
Values may be sent and summed in bfloat16 or wider, within the bound.
A program may use at most 64 MiB of HBM per device.

v0:
```python
import jax
import jax.numpy as jnp
from jax import lax
from jax.sharding import PartitionSpec as P


def shards(context, cotangent, out_weight):
    groups = lax.axis_size(("batch", "seq"))
    members = lax.axis_size("mp")
    split_rows = lax.all_to_all(context, "mp", split_axis=0, concat_axis=1, tiled=True)
    block_rows = lax.all_to_all(
        split_rows, ("batch", "seq"), split_axis=1, concat_axis=0, tiled=True
    )
    feature_block = lax.all_gather(block_rows, "mp", axis=0, tiled=True)
    all_cotangent = lax.all_gather(cotangent, ("batch", "seq"), axis=0, tiled=True)
    share = split_rows.shape[0]
    shaped_context = feature_block.reshape(members, groups, share, feature_block.shape[1])
    shaped_cotangent = all_cotangent.reshape(groups, members, share, all_cotangent.shape[1])
    grad_weight = lax.dot_general(
        shaped_context,
        shaped_cotangent,
        (((0, 1, 2), (1, 0, 2)), ((), ())),
        preferred_element_type=jnp.float32,
    )
    partial_input = lax.dot_general(
        cotangent, out_weight, (((1,), (1,)), ((), ())), preferred_element_type=jnp.float32
    )
    grad_context = lax.psum_scatter(partial_input, "mp", scatter_dimension=1, tiled=True).astype(
        jnp.bfloat16
    )
    return (grad_weight, grad_context)


def solution(mesh):
    return jax.shard_map(
        shards,
        mesh=mesh,
        in_specs=(P(("batch", "seq"), "mp"), P(("batch", "seq"), "mp"), P(None, "mp")),
        out_specs=(P(("batch", "seq"), "mp"), P(("batch", "seq"), "mp")),
        check_vma=False,
    )
```

profile of v0, /device:TPU:0, one launch (start us, length us, event | category | flops | bytes accessed | tf_op | source)
XLA Modules:
  0.0 176.4 jit_solution(15021152544623179522)
XLA Ops:
  7.2 0.0 copy-start
  7.2 0.0 all-gather.3.cloned.1.call-start
  7.2 18.2 %all_to_all.35 = bf16[4,32,1536]{2,1,0:T(8,128)(2,1)S(1)} all-to-all(bf16[4,32,1536]{2,1,0:T(8,128)(2,1)} %bitcast.16), channel_id=1, replica_groups=mesh['batch'=2,'seq'=4,'mp'=4] {'mp'}, dimensions={0} | all-to-all | bytes 786432 | tf_op jit(solution)/shard_map/all_to_all | solution.py:10
  25.4 0.3 copy.10
  25.7 0.1 all_to_all.29
  25.8 0.1 copy.11
  25.9 11.6 %all_to_all.36 = bf16[32,8,768]{2,0,1:T(8,128)(2,1)} all-to-all(bf16[32,8,768]{2,0,1:T(8,128)(2,1)S(1)} %copy.11), channel_id=1, replica_groups=mesh['batch'=2,'seq'=4,'mp'=4] {'batch','seq'}, dimensions={1} | all-to-all | bytes 786432 | tf_op jit(solution)/shard_map/all_to_all | solution.py:11
  37.5 0.0 all-gather.3.cloned.1.call-update
  37.5 0.0 all-gather.5.cloned.1.call-start
  37.6 0.7 all-gather.5.cloned.1.call-update
  38.3 0.0 reduce-scatter.2.cloned.1.call-start
  38.3 0.0 copy-done
  38.3 14.6 %fusion.1 = f32[128,6144]{1,0:T(8,128)} fusion(bf16[128,1536]{1,0:T(8,128)(2,1)S(1)} %copy-done, bf16[6144,1536]{1,0:T(8,128)(2,1)} %param.5), kind=kOutput, calls=%fused_computation.2 | convolution fusion | flops 2415919104 | bytes 22413312 | tf_op jit(solution)/shard_map/dot_general | solution.py:25
  52.9 0.0 reduce-scatter.2.cloned.1.call-update
  52.9 19.4 %all-gather.3.cloned.1.call-done = bf16[1024,768]{1,0:T(8,128)(2,1)} async-done(((bf16[256,768]{1,0:T(8,128)(2,1)}), bf16[1024,768]{1,0:T(8,128)(2,1)}) %all-gather.3.cloned.1.call-update) | async-done | bytes 1572880 | tf_op jit(solution)/shard_map/all_gather | solution.py:14
  72.3 33.0 %all-gather.5.cloned.1.call-done = bf16[1024,1536]{1,0:T(8,128)(2,1)} async-done(((bf16[128,1536]{1,0:T(8,128)(2,1)}), bf16[1024,1536]{1,0:T(8,128)(2,1)}) %all-gather.5.cloned.1.call-update) | async-done | bytes 3145744 | tf_op jit(solution)/shard_map/all_gather | solution.py:15
  105.2 7.2 %convolution_bitcast_fusion = f32[768,1536]{1,0:T(8,128)} fusion(bf16[4,8,32,768]{3,2,1,0:T(8,128)(2,1)} %bitcast.18, bf16[8,4,32,1536]{3,2,1,0:T(8,128)(2,1)} %bitcast.17), kind=kOutput, calls=%fused_computation | convolution fusion | flops 2415919104 | bytes 9437184 | tf_op jit(solution)/shard_map/dot_general | solution.py:19
  112.4 55.5 %reduce-scatter.2.cloned.1.call-done = f32[128,1536]{1,0:T(8,128)} async-done(((f32[128,6144]{1,0:T(8,128)}), f32[128,1536]{1,0:T(8,128)}) %reduce-scatter.2.cloned.1.call-update) | async-done | bytes 786448 | tf_op jit(solution)/shard_map/reduce_scatter | solution.py:28
  168.0 1.9 %convert_element_type.3 = bf16[128,1536]{1,0:T(8,128)(2,1)} convert(f32[128,1536]{1,0:T(8,128)} %reduce-scatter.2.cloned.1.call-done) | non-fusion elementwise | flops 196608 | bytes 1179648 | tf_op jit(solution)/shard_map/convert_element_type | solution.py:28
Async XLA Ops:
  7.2 31.2 %copy-start = (bf16[128,1536]{1,0:T(8,128)(2,1)S(1)}, bf16[128,1536]{1,0:T(8,128)(2,1)}, u32[]{:S(2)}) copy-start(bf16[128,1536]{1,0:T(8,128)(2,1)} %param.4) | copy-start | bytes 1179652
  7.2 65.1 %all-gather.3.cloned.1.call-start = ((), (), s32[]{:S(2)}) async-start(), calls=%async_computation.3 | async-start | bytes 1966080 | tf_op jit(solution)/shard_map/all_gather | solution.py:14
  37.5 67.7 %all-gather.5.cloned.1.call-start = ((), (), s32[]{:S(2)}) async-start(), calls=%async_computation.4 | async-start | bytes 3538944 | tf_op jit(solution)/shard_map/all_gather | solution.py:15
  38.3 129.7 %reduce-scatter.2.cloned.1.call-start = ((), (), s32[]{:S(2)}) async-start(), calls=%async_computation.5 | async-start | bytes 3932160 | tf_op jit(solution)/shard_map/reduce_scatter | solution.py:28
Sparse Core Ops, SparseCore 0:
  37.6 34.5 all-gather.2
  74.2 31.0 all-gather.4
  107.6 60.3 reduce-scatter.1
where the time goes:
time: 177 us; the launch traced here: 176 us
  waiting for transfers between devices  109 us (62%)
  blocking collectives  29.8 us (17%)
  matrix products  21.8 us (12%)
  between operations  13.8 us (8%)
  other arithmetic  1.92 us (1%)
    reduce_scatter x1, waiting for transfers between devices, shards(): lax.psum_scatter(partial_input, 'mp', scatter_dimension=1, tiled=True)  55.5 us
    all_gather x1, waiting for transfers between devices, shards(): lax.all_gather(cotangent, ('batch', 'seq'), axis=0, tiled=True)  33 us
    all_gather x1, waiting for transfers between devices, shards(): feature_block = lax.all_gather(block_rows, 'mp', axis=0, tiled=True)  19.4 us
    all_to_all x1, blocking collectives, shards(): lax.all_to_all(context, 'mp', split_axis=0, concat_axis=1, tiled=True)  18.2 us
    dot_general x1, matrix products, shards(): lax.dot_general(cotangent, out_weight, (((1,), (1,)), ((), ())), preferre...  14.6 us
    all_to_all x1, blocking collectives, shards(): lax.all_to_all(split_rows, ('batch', 'seq'), split_axis=1, concat_axis=0,...  11.6 us
    dot_general x1, matrix products, shards(): lax.dot_general(shaped_context, shaped_cotangent, (((0, 1, 2), (1, 0, 2))...  7.19 us
  transfers between devices with their start and end apart: 3, of which 3 were waited for; matrix products, arithmetic and copies ran while one was open for 12% of the time, Pallas kernels for 0%

commit v1 on v0

--- a/solution.py
+++ b/solution.py
@@ -11,7 +11,12 @@
     block_rows = lax.all_to_all(
         split_rows, ("batch", "seq"), split_axis=1, concat_axis=0, tiled=True
     )
-    feature_block = lax.all_gather(block_rows, "mp", axis=0, tiled=True)
+    ring = [block_rows]
+    for hop in range(3):
+        ring.append(lax.ppermute(ring[-1], "mp", [(dev, (dev + 1) % 4) for dev in range(4)]))
+    feature_block = jnp.roll(
+        jnp.concatenate(ring[::-1], axis=0), (lax.axis_index("mp") + 1) * ring[0].shape[0], axis=0
+    )
     all_cotangent = lax.all_gather(cotangent, ("batch", "seq"), axis=0, tiled=True)
     share = split_rows.shape[0]
     shaped_context = feature_block.reshape(members, groups, share, feature_block.shape[1])

time: 177 us -> 137 us (0.77)
  waiting for transfers between devices: 109 us -> 53.3 us
  blocking collectives: 29.8 us -> 39.8 us
  starting transfers between devices: 0.12 us -> 4.25 us
  between operations: 13.8 us -> 15.6 us
    reduce_scatter x1, waiting for transfers between devices: 55.5 us -> 0.01 us  [shards(): lax.psum_scatter(partial_input, 'mp', scatter_dimension=1, tiled=True)]
    ppermute x0 -> x3, waiting for transfers between devices: none -> 52.6 us  [shards(): lax.ppermute(ring[-1], 'mp', [(dev, (dev + 1) % 4) for dev in range(4)])]
    all_gather x1, waiting for transfers between devices: 33 us -> 0.02 us  [shards(): lax.all_gather(cotangent, ('batch', 'seq'), axis=0, tiled=True)]
    all_gather x1 -> x0, waiting for transfers between devices: 19.4 us -> none  [shards(): feature_block = lax.all_gather(block_rows, 'mp', axis=0, tiled=True)]
    all_to_all x1, blocking collectives: 18.2 us -> 28.3 us  [shards(): lax.all_to_all(context, 'mp', split_axis=0, concat_axis=1, tiled=True)]
    ppermute x0 -> x3, starting transfers between devices: none -> 4.17 us  [shards(): lax.ppermute(ring[-1], 'mp', [(dev, (dev + 1) % 4) for dev in range(4)])]
  transfers between devices with their start and end apart: 3 -> 5, of which waited for: 3 -> 3; matrix products, arithmetic and copies ran while one was open for 12% -> 15% of each run, Pallas kernels for 0% -> 0%
where the time goes in v1:
time: 137 us
  waiting for transfers between devices  53.3 us (39%)
  blocking collectives  39.8 us (29%)
  matrix products  20.5 us (15%)
  between operations  15.6 us (11%)
  starting transfers between devices  4.25 us (3%)
  other arithmetic  1.92 us (1%)
  local copies, waits for them, and re-layouts  1.77 us (1%)
    ppermute x3, waiting for transfers between devices, shards(): lax.ppermute(ring[-1], 'mp', [(dev, (dev + 1) % 4) for dev in range(4)])  52.6 us
    all_to_all x1, blocking collectives, shards(): lax.all_to_all(context, 'mp', split_axis=0, concat_axis=1, tiled=True)  28.3 us
    dot_general x1, matrix products, shards(): lax.dot_general(cotangent, out_weight, (((1,), (1,)), ((), ())), preferre...  14.3 us
    all_to_all x1, blocking collectives, shards(): lax.all_to_all(split_rows, ('batch', 'seq'), split_axis=1, concat_axis=0,...  11.5 us
    dot_general x1, matrix products, shards(): lax.dot_general(shaped_context, shaped_cotangent, (((0, 1, 2), (1, 0, 2))...  6.16 us
    ppermute x3, starting transfers between devices, shards(): lax.ppermute(ring[-1], 'mp', [(dev, (dev + 1) % 4) for dev in range(4)])  4.17 us
  transfers between devices with their start and end apart: 5, of which 3 were waited for; matrix products, arithmetic and copies ran while one was open for 15% of the time, Pallas kernels for 0%

profile of v1, /device:TPU:0, one launch (start us, length us, event | category | flops | bytes accessed | tf_op | source)
XLA Modules:
  0.0 137.1 jit_solution(8129972238352895839)
XLA Ops:
  8.0 0.0 all-gather.2.cloned.1.call-start
  8.0 0.7 all-gather.2.cloned.1.call-update
  8.7 0.0 reduce-scatter.2.cloned.1.call-start
  8.8 14.3 %fusion.1 = f32[128,6144]{1,0:T(8,128)} fusion(bf16[128,1536]{1,0:T(8,128)(2,1)} %param.4, bf16[6144,1536]{1,0:T(8,128)(2,1)} %param.5), kind=kOutput, calls=%fused_computation.11 | convolution fusion | flops 2415919104 | bytes 22413312 | tf_op jit(solution)/shard_map/dot_general | solution.py:30
  23.1 0.0 copy-start
  23.1 0.0 reduce-scatter.2.cloned.1.call-update
  23.1 1.0 copy-done
  24.1 28.3 %all_to_all.35 = bf16[4,32,1536]{2,1,0:T(8,128)(2,1)S(1)} all-to-all(bf16[4,32,1536]{2,1,0:T(8,128)(2,1)S(1)} %bitcast.19), channel_id=1, replica_groups=mesh['batch'=2,'seq'=4,'mp'=4] {'mp'}, dimensions={0} | all-to-all | bytes 786432 | tf_op jit(solution)/shard_map/all_to_all | solution.py:10
  52.3 0.3 copy.10
  52.6 0.1 all_to_all.29
  52.7 0.1 copy.11
  52.8 11.5 %all_to_all.36 = bf16[32,8,768]{2,0,1:T(8,128)(2,1)S(1)} all-to-all(bf16[32,8,768]{2,0,1:T(8,128)(2,1)S(1)} %copy.11), channel_id=1, replica_groups=mesh['batch'=2,'seq'=4,'mp'=4] {'batch','seq'}, dimensions={1} | all-to-all | bytes 786432 | tf_op jit(solution)/shard_map/all_to_all | solution.py:11
  64.3 0.0 collective-permute-start
  64.3 21.9 %collective-permute-done = bf16[256,768]{1,0:T(8,128)(2,1)S(1)} collective-permute-done((bf16[256,768]{1,0:T(8,128)(2,1)S(1)}, bf16[256,768]{1,0:T(8,128)(2,1)S(1)}, u32[]{:S(2)}, u32[]{:S(2)}) %collective-permute-start) | collective-permute-done | bytes 393248 | tf_op jit(solution)/shard_map/ppermute | solution.py:16
  86.2 4.2 %collective-permute-start.1 = (bf16[256,768]{1,0:T(8,128)(2,1)S(1)}, bf16[256,768]{1,0:T(8,128)(2,1)S(1)}, u32[]{:S(2)}, u32[]{:S(2)}) collective-permute-start(bf16[256,768]{1,0:T(8,128)(2,1)S(1)} %collective-permute-done), channel_id=1, source_target_pairs={{0,1},{1,2},{2,3},{3,0},{4,5},{5,6},{6,7},{7,4},{8,9},{9,10},{10,1... | collective-permute-start | bytes 1179656 | tf_op jit(solution)/shard_map/ppermute | solution.py:16
  90.4 17.9 %collective-permute-done.1 = bf16[256,768]{1,0:T(8,128)(2,1)S(1)} collective-permute-done((bf16[256,768]{1,0:T(8,128)(2,1)S(1)}, bf16[256,768]{1,0:T(8,128)(2,1)S(1)}, u32[]{:S(2)}, u32[]{:S(2)}) %collective-permute-start.1) | collective-permute-done | bytes 393248 | tf_op jit(solution)/shard_map/ppermute | solution.py:16
  108.3 0.0 collective-permute-start.2
  108.3 12.8 %collective-permute-done.2 = bf16[256,768]{1,0:T(8,128)(2,1)S(1)} collective-permute-done((bf16[256,768]{1,0:T(8,128)(2,1)S(1)}, bf16[256,768]{1,0:T(8,128)(2,1)S(1)}, u32[]{:S(2)}, u32[]{:S(2)}) %collective-permute-start.2) | collective-permute-done | bytes 393248 | tf_op jit(solution)/shard_map/ppermute | solution.py:16
  121.4 0.1 constant_dynamic-slice_fusion
  121.5 0.0 all-gather.2.cloned.1.call-done
  121.5 6.2 %convolution_bitcast_fusion = f32[768,1536]{1,0:T(8,128)} fusion(bf16[4,8,32,768]{3,2,1,0:T(8,128)(2,1)S(1)} %bitcast.18, bf16[8,4,32,1536]{3,2,1,0:T(8,128)(2,1)} %bitcast.20), kind=kOutput, calls=%fused_computation | convolution fusion | flops 2415919104 | bytes 9437184 | tf_op jit(solution)/shard_map/dot_general | solution.py:24
  127.7 0.0 reduce-scatter.2.cloned.1.call-done
  127.7 1.9 %convert_element_type.3 = bf16[128,1536]{1,0:T(8,128)(2,1)} convert(f32[128,1536]{1,0:T(8,128)} %reduce-scatter.2.cloned.1.call-done) | non-fusion elementwise | flops 196608 | bytes 1179648 | tf_op jit(solution)/shard_map/convert_element_type | solution.py:33
  (8 shorter events, 0.2 us)
Async XLA Ops:
  8.0 113.5 %all-gather.2.cloned.1.call-start = ((), (), s32[]{:S(2)}) async-start(), calls=%async_computation.3 | async-start | bytes 3538944 | tf_op jit(solution)/shard_map/all_gather | solution.py:20
  8.7 119.0 %reduce-scatter.2.cloned.1.call-start = ((), (), s32[]{:S(2)}) async-start(), calls=%async_computation.4 | async-start | bytes 3932160 | tf_op jit(solution)/shard_map/reduce_scatter | solution.py:33
  23.1 1.0 copy-start
  64.3 21.9 %collective-permute-start = (bf16[256,768]{1,0:T(8,128)(2,1)S(1)}, bf16[256,768]{1,0:T(8,128)(2,1)S(1)}, u32[]{:S(2)}, u32[]{:S(2)}) collective-permute-start(bf16[256,768]{1,0:T(8,128)(2,1)S(1)} %bitcast.14), channel_id=1, source_target_pairs={{0,1},{1,2},{2,3},{3,0},{4,5},{5,6},{6,7},{7,4},{8,9},{9,10},{10,1... | collective-permute-start | bytes 1179656 | tf_op jit(solution)/shard_map/ppermute | solution.py:16
  86.2 22.1 %collective-permute-start.1 = (bf16[256,768]{1,0:T(8,128)(2,1)S(1)}, bf16[256,768]{1,0:T(8,128)(2,1)S(1)}, u32[]{:S(2)}, u32[]{:S(2)}) collective-permute-start(bf16[256,768]{1,0:T(8,128)(2,1)S(1)} %collective-permute-done), channel_id=1, source_target_pairs={{0,1},{1,2},{2,3},{3,0},{4,5},{5,6},{6,7},{7,4},{8,9},{9,10},{10,1... | collective-permute-start | bytes 1179656 | tf_op jit(solution)/shard_map/ppermute | solution.py:16
  108.3 12.8 %collective-permute-start.2 = (bf16[256,768]{1,0:T(8,128)(2,1)S(1)}, bf16[256,768]{1,0:T(8,128)(2,1)S(1)}, u32[]{:S(2)}, u32[]{:S(2)}) collective-permute-start(bf16[256,768]{1,0:T(8,128)(2,1)S(1)} %collective-permute-done.1), channel_id=1, source_target_pairs={{0,1},{1,2},{2,3},{3,0},{4,5},{5,6},{6,7},{7,4},{8,9},{9,10},{10,1... | collective-permute-start | bytes 1179656 | tf_op jit(solution)/shard_map/ppermute | solution.py:16
Sparse Core Ops, SparseCore 0:
  10.7 34.9 all-gather.1
Sparse Core Ops, SparseCore 1:
  23.2 80.9 reduce-scatter.1

commit v2 on v0

--- a/solution.py
+++ b/solution.py
@@ -7,7 +7,10 @@
 def shards(context, cotangent, out_weight):
     groups = lax.axis_size(("batch", "seq"))
     members = lax.axis_size("mp")
-    split_rows = lax.all_to_all(context, "mp", split_axis=0, concat_axis=1, tiled=True)
+    split_rows = jnp.concatenate(
+        lax.all_to_all(jnp.stack(jnp.split(context, lax.axis_size("mp"), axis=0)), "mp", 0, 0),
+        axis=1,
+    )
     block_rows = lax.all_to_all(
         split_rows, ("batch", "seq"), split_axis=1, concat_axis=0, tiled=True
     )

time: 177 us -> 178 us (level)
  no operation moved by 1% of the time
where the time goes in v2:
time: 178 us; the launch traced here: 177 us
  waiting for transfers between devices  109 us (61%)
  blocking collectives  29.5 us (17%)
  matrix products  21.7 us (12%)
  between operations  13.8 us (8%)
  other arithmetic  1.97 us (1%)
    reduce_scatter x1, waiting for transfers between devices, shards(): lax.psum_scatter(partial_input, 'mp', scatter_dimension=1, tiled=True)  55.5 us
    all_gather x1, waiting for transfers between devices, shards(): lax.all_gather(cotangent, ('batch', 'seq'), axis=0, tiled=True)  33 us
    all_gather x1, waiting for transfers between devices, shards(): feature_block = lax.all_gather(block_rows, 'mp', axis=0, tiled=True)  19.4 us
    all_to_all x1, blocking collectives, shards(): lax.all_to_all(jnp.stack(jnp.split(context, lax.axis_size('mp'), axis=0))...  17.8 us
    dot_general x1, matrix products, shards(): lax.dot_general(cotangent, out_weight, (((1,), (1,)), ((), ())), preferre...  14.5 us
    all_to_all x1, blocking collectives, shards(): lax.all_to_all(split_rows, ('batch', 'seq'), split_axis=1, concat_axis=0,...  11.6 us
    dot_general x1, matrix products, shards(): lax.dot_general(shaped_context, shaped_cotangent, (((0, 1, 2), (1, 0, 2))...  7.19 us
  transfers between devices with their start and end apart: 3, of which 3 were waited for; matrix products, arithmetic and copies ran while one was open for 12% of the time, Pallas kernels for 0%

profile of v2, /device:TPU:0, one launch (start us, length us, event | category | flops | bytes accessed | tf_op | source)
XLA Modules:
  0.0 177.3 jit_solution(8491093557890151525)
XLA Ops:
  7.2 0.0 copy-start
  7.2 0.0 all-gather.3.cloned.1.call-start
  7.2 1.1 slice_bitcast_fusion.3
  8.3 0.1 pad_maximum_fusion
  8.4 17.8 %all_to_all.24 = bf16[4,32,1536]{2,1,0:T(8,128)(2,1)S(1)} all-to-all(bf16[4,32,1536]{2,1,0:T(8,128)(2,1)S(1)} %pad_maximum_fusion), channel_id=1, replica_groups=mesh['batch'=2,'seq'=4,'mp'=4] {'mp'}, dimensions={0} | all-to-all | bytes 786432 | tf_op jit(solution)/shard_map/all_to_all | solution.py:11
  26.2 0.3 copy.10
  26.5 0.1 all_to_all.18
  26.6 0.1 copy.11
  26.7 11.6 %all_to_all.25 = bf16[32,8,768]{2,0,1:T(8,128)(2,1)} all-to-all(bf16[32,8,768]{2,0,1:T(8,128)(2,1)S(1)} %copy.11), channel_id=1, replica_groups=mesh['batch'=2,'seq'=4,'mp'=4] {'batch','seq'}, dimensions={1} | all-to-all | bytes 786432 | tf_op jit(solution)/shard_map/all_to_all | solution.py:14
  38.3 0.0 all-gather.3.cloned.1.call-update
  38.4 0.0 all-gather.5.cloned.1.call-start
  38.4 0.7 all-gather.5.cloned.1.call-update
  39.1 0.0 reduce-scatter.2.cloned.1.call-start
  39.2 0.0 copy-done
  39.2 14.5 %fusion.1 = f32[128,6144]{1,0:T(8,128)} fusion(bf16[128,1536]{1,0:T(8,128)(2,1)S(1)} %copy-done, bf16[6144,1536]{1,0:T(8,128)(2,1)} %param.5), kind=kOutput, calls=%fused_computation.7 | convolution fusion | flops 2415919104 | bytes 22413312 | tf_op jit(solution)/shard_map/dot_general | solution.py:28
  53.7 0.0 reduce-scatter.2.cloned.1.call-update
  53.7 19.4 %all-gather.3.cloned.1.call-done = bf16[1024,768]{1,0:T(8,128)(2,1)} async-done(((bf16[256,768]{1,0:T(8,128)(2,1)}), bf16[1024,768]{1,0:T(8,128)(2,1)}) %all-gather.3.cloned.1.call-update) | async-done | bytes 1572880 | tf_op jit(solution)/shard_map/all_gather | solution.py:17
  73.1 33.0 %all-gather.5.cloned.1.call-done = bf16[1024,1536]{1,0:T(8,128)(2,1)} async-done(((bf16[128,1536]{1,0:T(8,128)(2,1)}), bf16[1024,1536]{1,0:T(8,128)(2,1)}) %all-gather.5.cloned.1.call-update) | async-done | bytes 3145744 | tf_op jit(solution)/shard_map/all_gather | solution.py:18
  106.1 7.2 %convolution_bitcast_fusion = f32[768,1536]{1,0:T(8,128)} fusion(bf16[4,8,32,768]{3,2,1,0:T(8,128)(2,1)} %bitcast.24, bf16[8,4,32,1536]{3,2,1,0:T(8,128)(2,1)} %bitcast.23), kind=kOutput, calls=%fused_computation | convolution fusion | flops 2415919104 | bytes 9437184 | tf_op jit(solution)/shard_map/dot_general | solution.py:22
  113.3 55.5 %reduce-scatter.2.cloned.1.call-done = f32[128,1536]{1,0:T(8,128)} async-done(((f32[128,6144]{1,0:T(8,128)}), f32[128,1536]{1,0:T(8,128)}) %reduce-scatter.2.cloned.1.call-update) | async-done | bytes 786448 | tf_op jit(solution)/shard_map/reduce_scatter | solution.py:31
  168.8 1.9 %convert_element_type.3 = bf16[128,1536]{1,0:T(8,128)(2,1)} convert(f32[128,1536]{1,0:T(8,128)} %reduce-scatter.2.cloned.1.call-done) | non-fusion elementwise | flops 196608 | bytes 1179648 | tf_op jit(solution)/shard_map/convert_element_type | solution.py:31
Async XLA Ops:
  7.2 32.0 %copy-start = (bf16[128,1536]{1,0:T(8,128)(2,1)S(1)}, bf16[128,1536]{1,0:T(8,128)(2,1)}, u32[]{:S(2)}) copy-start(bf16[128,1536]{1,0:T(8,128)(2,1)} %param.4) | copy-start | bytes 1179652
  7.2 65.9 %all-gather.3.cloned.1.call-start = ((), (), s32[]{:S(2)}) async-start(), calls=%async_computation.3 | async-start | bytes 1966080 | tf_op jit(solution)/shard_map/all_gather | solution.py:17
  38.4 67.7 %all-gather.5.cloned.1.call-start = ((), (), s32[]{:S(2)}) async-start(), calls=%async_computation.4 | async-start | bytes 3538944 | tf_op jit(solution)/shard_map/all_gather | solution.py:18
  39.1 129.7 %reduce-scatter.2.cloned.1.call-start = ((), (), s32[]{:S(2)}) async-start(), calls=%async_computation.5 | async-start | bytes 3932160 | tf_op jit(solution)/shard_map/reduce_scatter | solution.py:31
Sparse Core Ops, SparseCore 0:
  38.5 34.5 all-gather.2
  75.0 31.0 all-gather.4
  108.4 60.3 reduce-scatter.1
